TPU v7x, 512 devices: a whole 4x8x8 slice. The times are simulated.
512 devices in a mesh: term: 8 (over z), sector: 64 (over x, y, core).
Axes of the slice: x: 4, y: 8, z: 8, core: 2. Of those that a mesh axis runs over, the one named last changes fastest.
Arguments:
- wave_tiles: bfloat16 [1024, 2, 128, 128], P('sector'), may hold values from -6 to 6
- left_env: bfloat16 [8, 64, 128, 128], P('term', 'sector'), may hold values from -0.5 to 0.5
- right_env: bfloat16 [8, 64, 128, 128], P('term', 'sector'), may hold values from -0.5 to 0.5
- send_list: int32 [64, 128], P('sector'), may hold values from -1 to 15, as said below
- left_tasks: int32 [8, 64, 96, 3], P('term', 'sector'), may hold values from 0 to 127, as said below
- right_tasks: int32 [8, 64, 256, 3], P('term', 'sector'), may hold values from 0 to 63, as said below
Outputs:
- sigma: float32 [1024, 2, 128, 128], P('sector', None, 'term')
Inputs may be any that keep to these rules, and one draw needn't show every extreme that they name: send_list[s, o * 2 + c] is a tile index local to sender s, or -1 for an empty slot; some owner drawn from the seed receives a full 2 tiles from every sender. `left_tasks`: entries 0, 1, 2 lie below 64, 128 and 32. `right_tasks`: entries 0, 1, 2 lie below 32, 64 and 16.
All inputs are finite; a program needn't handle non-finite values.
Results may differ from a plain program's by a relative error of at most 0.0029.
Values may be sent and summed in bfloat16 or wider, within the bound.
A program may use at most 128 MiB of HBM per device.

v0:
```python
import math
import jax
import jax.numpy as jnp
from jax import lax
from jax.sharding import PartitionSpec as P

INTER_TILES = 32


def run_tasks(tasks, first_tiles, second_tiles, contract, count):
    block = math.gcd(tasks.shape[0], 32)
    shape = (count,) + tuple(contract(first_tiles[:1], second_tiles[:1]).shape[1:])

    def step(turn, total):
        rows = lax.dynamic_slice_in_dim(tasks, turn * block, block, 0)
        first = jnp.take(first_tiles, rows[:, 0], axis=0)
        second = jnp.take(second_tiles, rows[:, 1], axis=0)
        return total.at[rows[:, 2]].add(contract(first, second))

    return lax.fori_loop(0, tasks.shape[0] // block, step, jnp.zeros(shape, jnp.float32))


def left_product(env_part, wave_part):
    return jnp.einsum("bij,bvjk->bvik", env_part, wave_part, preferred_element_type=jnp.float32)


def right_product(inter_part, env_part):
    return jnp.einsum("bvij,bjk->bvik", inter_part, env_part, preferred_element_type=jnp.float32)


def shards(wave_tiles, left_env, right_env, send_list, left_tasks, right_tasks):
    env_left, env_right = (
        lax.all_gather(left_env, "sector", axis=1, tiled=True),
        lax.all_gather(right_env, "sector", axis=1, tiled=True),
    )
    env_left = env_left[0]
    env_right = env_right[0]
    slot_list = send_list[0]
    live = slot_list >= 0
    picked = jnp.take(wave_tiles, jnp.maximum(slot_list, 0), axis=0)
    outgoing = jnp.where(live[:, None, None, None], picked, jnp.zeros((), jnp.bfloat16))
    tile_dim = wave_tiles.shape[2]
    groups = lax.axis_size("term")
    share = tile_dim // groups
    received = lax.all_to_all(outgoing, "sector", split_axis=0, concat_axis=0, tiled=True)
    inter = run_tasks(left_tasks[0, 0], env_left, received, left_product, INTER_TILES).astype(
        jnp.bfloat16
    )
    partial_value = run_tasks(
        right_tasks[0, 0], inter, env_right, right_product, wave_tiles.shape[0]
    )
    summed = lax.psum(partial_value, "term")
    return lax.dynamic_slice_in_dim(summed, lax.axis_index("term") * share, share, 2)


def solution(mesh):
    in_specs = (
        P("sector", None, None, None),
        P("term", "sector", None, None),
        P("term", "sector", None, None),
        P("sector", None),
        P("term", "sector", None, None),
        P("term", "sector", None, None),
    )
    out_specs = P("sector", None, "term", None)
    return jax.shard_map(shards, mesh=mesh, in_specs=in_specs, out_specs=out_specs, check_vma=False)
```

profile of v0, /device:TPU:2, one launch (start us, length us, event | category | flops | bytes accessed | tf_op | source)
XLA Modules:
  0.0 562.8 jit_solution(14975568767976974510)
XLA Ops:
  8.0 6.5 %gather_fusion.4 = bf16[128,2,128,128]{3,2,1,0:T(8,128)(2,1)} fusion(bf16[16,2,128,128]{3,2,1,0:T(8,128)(2,1)S(1)} %copy-done, s32[1024]{0:T(1024)S(1)} %pad_clamp_fusion.4), kind=kCustom, calls=%fused_computation.4 | custom fusion | bytes 16777728 | tf_op jit(solution)/shard_map/jit(_take)/gather | solution.py:40
  14.5 7.5 %select_select_fusion = bf16[128,2,128,128]{3,2,1,0:T(8,128)(2,1)} fusion(bf16[128,2,128,128]{3,2,1,0:T(8,128)(2,1)} %gather_fusion.4, pred[128]{0:T(512)(128)(4,1)S(1)} %get-tuple-element.225, pred[128]{0:T(512)(128)(4,1)S(1)} %get-tuple-element.224), kind=kLoop, calls=%fused_computation.45 | loop fusion | flops 8388608 | bytes 16777472 | tf_op jit(solution)/shard_map/jit(_where)/select_n | solution.py:41
  22.0 11.3 %all-to-all-start = ((bf16[128,2,128,128]{3,2,1,0:T(8,128)(2,1)}), bf16[128,2,128,128]{3,2,1,0:T(8,128)(2,1)}, u32[]{:S(2)}, u32[]{:S(2)}) async-start(bf16[128,2,128,128]{3,2,1,0:T(8,128)(2,1)} %select_select_fusion), calls=%async_computation | async-start | bytes 16777216 | tf_op jit(solution)/shard_map/all_to_all | solution.py:45
  34.8 102.3 %all-gather.3.cloned.1.call-done = bf16[1,64,128,128]{3,2,0,1:T(8,128)(2,1)} async-done(((bf16[1,1,128,128]{3,2,0,1:T(8,128)(2,1)}), bf16[1,64,128,128]{3,2,0,1:T(8,128)(2,1)}) %all-gather.3.cloned.1.call-update) | async-done | bytes 2097168 | tf_op jit(solution)/shard_map/all_gather | solution.py:33
  137.1 90.6 %all-to-all-done = bf16[128,2,128,128]{3,2,1,0:T(8,128)(2,1)} async-done(((bf16[128,2,128,128]{3,2,1,0:T(8,128)(2,1)}), bf16[128,2,128,128]{3,2,1,0:T(8,128)(2,1)}, u32[]{:S(2)}, u32[]{:S(2)}) %all-to-all-start) | async-done | bytes 8388640 | tf_op jit(solution)/shard_map/all_to_all | solution.py:45
  230.2 82.3 %while.26 = (s32[]{:T(128)}, f32[32,2,128,128]{3,2,1,0:T(8,128)}, s32[96,3]{0,1:T(4,128)S(1)}, bf16[128,2,128,128]{3,2,1,0:T(8,128)(2,1)}, bf16[64,128,128]{2,1,...) while((s32[]{:T(128)}, f32[32,2,128,128]{3,2,1,0:T(8,128)}, s32[96,3]{0,1:T(4,128)S(1)}, ...), condition=%wide.region_2.4_spmd, body=%wide.region_0.3_spmd.sunk | while | flops 271059520 | bytes 34613776 | solution.py:20
  242.1 5.6 copy.23
  247.7 10.1 %scatter_fusion = f32[32,2,128,128]{3,2,1,0:T(8,128)} fusion(f32[32,2,128,128]{3,2,1,0:T(8,128)} %get-tuple-element.314, s32[32]{0:T(128)S(1)} %get-tuple-element.291, f32[32,2,128,128]{3,2,1,0:T(8,128)} %copy.23), kind=kCustom, calls=%fused_computation.5.clone.1 | custom fusion | flops 1048576 | bytes 12583040 | tf_op jit(solution)/shard_map/while/body/eval_jaxpr/scatter-add | solution.py:18
  269.6 5.6 copy.23
  275.2 9.9 %scatter_fusion = f32[32,2,128,128]{3,2,1,0:T(8,128)} fusion(f32[32,2,128,128]{3,2,1,0:T(8,128)} %get-tuple-element.314, s32[32]{0:T(128)S(1)} %get-tuple-element.291, f32[32,2,128,128]{3,2,1,0:T(8,128)} %copy.23), kind=kCustom, calls=%fused_computation.5.clone.1 | custom fusion | flops 1048576 | bytes 12583040 | tf_op jit(solution)/shard_map/while/body/eval_jaxpr/scatter-add | solution.py:18
  296.9 5.6 copy.23
  302.6 9.9 %scatter_fusion = f32[32,2,128,128]{3,2,1,0:T(8,128)} fusion(f32[32,2,128,128]{3,2,1,0:T(8,128)} %get-tuple-element.314, s32[32]{0:T(128)S(1)} %get-tuple-element.291, f32[32,2,128,128]{3,2,1,0:T(8,128)} %copy.23), kind=kCustom, calls=%fused_computation.5.clone.1 | custom fusion | flops 1048576 | bytes 12583040 | tf_op jit(solution)/shard_map/while/body/eval_jaxpr/scatter-add | solution.py:18
  316.6 145.3 %while.27 = (s32[]{:T(128)}, f32[16,2,128,128]{3,2,1,0:T(8,128)S(1)}, s32[256,3]{0,1:T(4,128)S(1)}, bf16[32,2,128,128]{3,2,1,0:T(8,128)(2,1)}, bf16[64,128,128]{...) while((s32[]{:T(128)}, f32[16,2,128,128]{3,2,1,0:T(8,128)S(1)}, ...), condition=%wide.region_5.7_spmd, body=%wide.region_3.6_spmd.sunk | while | flops 271059520 | bytes 26225168 | solution.py:20
  323.7 4.6 fusion.34
  328.3 6.5 %scatter_fusion.1 = f32[16,2,128,128]{3,2,1,0:T(8,128)S(1)} fusion(f32[16,2,128,128]{3,2,1,0:T(8,128)S(1)} %get-tuple-element.341, s32[32]{0:T(128)S(1)} %get-tuple-element.300, f32[32,2,128,128]{3,2,1,0:T(8,128)} %fusion.34), kind=kCustom, calls=%fused_computation.6.clone.1 | custom fusion | flops 1048576 | bytes 12583040 | tf_op jit(solution)/shard_map/while/body/eval_jaxpr/scatter-add | solution.py:18
  346.5 6.5 %scatter_fusion.1 = f32[16,2,128,128]{3,2,1,0:T(8,128)S(1)} fusion(f32[16,2,128,128]{3,2,1,0:T(8,128)S(1)} %get-tuple-element.341, s32[32]{0:T(128)S(1)} %get-tuple-element.300, f32[32,2,128,128]{3,2,1,0:T(8,128)} %fusion.34), kind=kCustom, calls=%fused_computation.6.clone.1 | custom fusion | flops 1048576 | bytes 12583040 | tf_op jit(solution)/shard_map/while/body/eval_jaxpr/scatter-add | solution.py:18
  364.6 6.5 %scatter_fusion.1 = f32[16,2,128,128]{3,2,1,0:T(8,128)S(1)} fusion(f32[16,2,128,128]{3,2,1,0:T(8,128)S(1)} %get-tuple-element.341, s32[32]{0:T(128)S(1)} %get-tuple-element.300, f32[32,2,128,128]{3,2,1,0:T(8,128)} %fusion.34), kind=kCustom, calls=%fused_computation.6.clone.1 | custom fusion | flops 1048576 | bytes 12583040 | tf_op jit(solution)/shard_map/while/body/eval_jaxpr/scatter-add | solution.py:18
  382.8 6.5 %scatter_fusion.1 = f32[16,2,128,128]{3,2,1,0:T(8,128)S(1)} fusion(f32[16,2,128,128]{3,2,1,0:T(8,128)S(1)} %get-tuple-element.341, s32[32]{0:T(128)S(1)} %get-tuple-element.300, f32[32,2,128,128]{3,2,1,0:T(8,128)} %fusion.34), kind=kCustom, calls=%fused_computation.6.clone.1 | custom fusion | flops 1048576 | bytes 12583040 | tf_op jit(solution)/shard_map/while/body/eval_jaxpr/scatter-add | solution.py:18
  400.9 6.5 %scatter_fusion.1 = f32[16,2,128,128]{3,2,1,0:T(8,128)S(1)} fusion(f32[16,2,128,128]{3,2,1,0:T(8,128)S(1)} %get-tuple-element.341, s32[32]{0:T(128)S(1)} %get-tuple-element.300, f32[32,2,128,128]{3,2,1,0:T(8,128)} %fusion.34), kind=kCustom, calls=%fused_computation.6.clone.1 | custom fusion | flops 1048576 | bytes 12583040 | tf_op jit(solution)/shard_map/while/body/eval_jaxpr/scatter-add | solution.py:18
  419.1 6.5 %scatter_fusion.1 = f32[16,2,128,128]{3,2,1,0:T(8,128)S(1)} fusion(f32[16,2,128,128]{3,2,1,0:T(8,128)S(1)} %get-tuple-element.341, s32[32]{0:T(128)S(1)} %get-tuple-element.300, f32[32,2,128,128]{3,2,1,0:T(8,128)} %fusion.34), kind=kCustom, calls=%fused_computation.6.clone.1 | custom fusion | flops 1048576 | bytes 12583040 | tf_op jit(solution)/shard_map/while/body/eval_jaxpr/scatter-add | solution.py:18
  432.7 4.6 fusion.34
  437.2 6.5 %scatter_fusion.1 = f32[16,2,128,128]{3,2,1,0:T(8,128)S(1)} fusion(f32[16,2,128,128]{3,2,1,0:T(8,128)S(1)} %get-tuple-element.341, s32[32]{0:T(128)S(1)} %get-tuple-element.300, f32[32,2,128,128]{3,2,1,0:T(8,128)} %fusion.34), kind=kCustom, calls=%fused_computation.6.clone.1 | custom fusion | flops 1048576 | bytes 12583040 | tf_op jit(solution)/shard_map/while/body/eval_jaxpr/scatter-add | solution.py:18
  455.4 6.5 %scatter_fusion.1 = f32[16,2,128,128]{3,2,1,0:T(8,128)S(1)} fusion(f32[16,2,128,128]{3,2,1,0:T(8,128)S(1)} %get-tuple-element.341, s32[32]{0:T(128)S(1)} %get-tuple-element.300, f32[32,2,128,128]{3,2,1,0:T(8,128)} %fusion.34), kind=kCustom, calls=%fused_computation.6.clone.1 | custom fusion | flops 1048576 | bytes 12583040 | tf_op jit(solution)/shard_map/while/body/eval_jaxpr/scatter-add | solution.py:18
  463.2 91.4 %all-reduce.2.cloned.1.call-done = f32[16,2,128,128]{3,2,1,0:T(8,128)} async-done(((f32[16,2,128,128]{3,2,1,0:T(8,128)}), f32[16,2,128,128]{3,2,1,0:T(8,128)}) %all-reduce.2.cloned.1.call-update) | async-done | bytes 2097168 | tf_op jit(solution)/shard_map/psum | solution.py:52
  (121 shorter events, 131.9 us)
Async XLA Ops:
  6.5 1.4 copy-start
  22.0 12.8 %copy-start.3 = (s32[1,1,96,3]{2,1,3,0:T(1,128)S(1)}, s32[1,1,96,3]{2,1,3,0:T(1,128)}, u32[]{:S(2)}) copy-start(s32[1,1,96,3]{2,1,3,0:T(1,128)} %param.16) | copy-start | bytes 3460
  22.0 12.8 %copy-start.2 = (s32[1,1,256,3]{2,1,3,0:T(1,128)S(1)}, s32[1,1,256,3]{2,1,3,0:T(1,128)}, u32[]{:S(2)}) copy-start(s32[1,1,256,3]{2,1,3,0:T(1,128)} %param.17) | copy-start | bytes 9220
  22.0 205.8 %all-to-all-start = ((bf16[128,2,128,128]{3,2,1,0:T(8,128)(2,1)}), bf16[128,2,128,128]{3,2,1,0:T(8,128)(2,1)}, u32[]{:S(2)}, u32[]{:S(2)}) async-start(bf16[128,2,128,128]{3,2,1,0:T(8,128)(2,1)} %select_select_fusion), calls=%async_computation | async-start | bytes 16777216 | tf_op jit(solution)/shard_map/all_to_all | solution.py:45
  33.3 103.9 %all-gather.3.cloned.1.call-start = ((), (), s32[]{:S(2)}) async-start(), calls=%async_computation.1 | async-start | bytes 2129920 | tf_op jit(solution)/shard_map/all_gather | solution.py:33
  34.0 282.4 %all-gather.5.cloned.1.call-start = ((), (), s32[]{:S(2)}) async-start(), calls=%async_computation.2 | async-start | bytes 2129920 | tf_op jit(solution)/shard_map/all_gather | solution.py:34
  34.8 519.8 %all-reduce.2.cloned.1.call-start = ((), (), s32[]{:S(2)}) async-start(), calls=%async_computation.3 | async-start | bytes 4194304 | tf_op jit(solution)/shard_map/psum | solution.py:52
  461.9 1.3 copy-start.1
Sparse Core Ops, SparseCore 0:
  37.5 99.6 all-gather.2
  140.5 95.8 all-gather.4
  463.3 91.2 all-reduce.1
where the time goes:
time: 565 us; the launch traced here: 563 us
  waiting for transfers between devices  286 us (51%)
  local copies, waits for them, and re-layouts  109 us (19%)
  other arithmetic  95 us (17%)
  matrix products  48.7 us (9%)
  between operations  13.2 us (2%)
  starting transfers between devices  11.4 us (2%)
    all_gather x1, waiting for transfers between devices, shards(): lax.all_gather(left_env, 'sector', axis=1, tiled=True)  102 us
    psum x1, waiting for transfers between devices, shards(): summed = lax.psum(partial_value, 'term')  91.4 us
    all_to_all x1, waiting for transfers between devices, shards(): lax.all_to_all(outgoing, 'sector', split_axis=0, concat_axis=0, tiled=True)  90.6 us
    scatter-add x11, other arithmetic, step(): return total.at[rows[:, 2]].add(contract(first, second))  81.8 us
    gather x11, local copies, waits for them, and re-layouts, step(): first = jnp.take(first_tiles, rows[:, 0], axis=0)  39.8 us
    gather x11, local copies, waits for them, and re-layouts, step(): second = jnp.take(second_tiles, rows[:, 1], axis=0)  38.9 us
    dot_general x8, matrix products, right_product(): jnp.einsum('bvij,bjk->bvik', inter_part, env_part, preferred_element_type...  36.6 us
    transpose x3, local copies, waits for them, and re-layouts, left_product(): jnp.einsum('bij,bvjk->bvik', env_part, wave_part, preferred_element_type=...  16.9 us
  transfers between devices with their start and end apart: 4, of which 3 were waited for; matrix products, arithmetic and copies ran while one was open for 16% of the time, Pallas kernels for 0%

commit v1 on v0

--- a/solution.py
+++ b/solution.py
@@ -5,6 +5,11 @@
 from jax.sharding import PartitionSpec as P
 
 INTER_TILES = 32
+
+
+def gather_over(value, name, along):
+    repeated = jnp.stack([value] * lax.axis_size(name))
+    return jnp.concatenate(lax.all_to_all(repeated, name, 0, 0), axis=along)
 
 
 def run_tasks(tasks, first_tiles, second_tiles, contract, count):
@@ -30,7 +35,7 @@
 
 def shards(wave_tiles, left_env, right_env, send_list, left_tasks, right_tasks):
     env_left, env_right = (
-        lax.all_gather(left_env, "sector", axis=1, tiled=True),
+        gather_over(left_env, "sector", 1),
         lax.all_gather(right_env, "sector", axis=1, tiled=True),
     )
     env_left = env_left[0]

time: 565 us -> 608 us (1.076)
  waiting for transfers between devices: 286 us -> 316 us
  starting transfers between devices: 11.4 us -> 18.6 us
    all_gather x1 -> x0, waiting for transfers between devices: 102 us -> none  [shards(): lax.all_gather(left_env, 'sector', axis=1, tiled=True)]
    all_to_all x1, waiting for transfers between devices: 90.6 us -> 189 us  [shards(): lax.all_to_all(outgoing, 'sector', split_axis=0, concat_axis=0, tiled=True)]
    all_to_all x0 -> x1, waiting for transfers between devices: none -> 35.4 us  [gather_over(): return jnp.concatenate(lax.all_to_all(repeated, name, 0, 0), axis=along)]
    all_to_all x0 -> x1, starting transfers between devices: none -> 10.8 us  [gather_over(): return jnp.concatenate(lax.all_to_all(repeated, name, 0, 0), axis=along)]
  transfers between devices with their start and end apart: 4 -> 4, of which waited for: 3 -> 3; matrix products, arithmetic and copies ran while one was open for 16% -> 17% of each run, Pallas kernels for 0% -> 0%
where the time goes in v1:
time: 608 us; the launch traced here: 606 us
  waiting for transfers between devices  316 us (52%)
  local copies, waits for them, and re-layouts  115 us (19%)
  other arithmetic  93.9 us (15%)
  matrix products  48.8 us (8%)
  starting transfers between devices  18.6 us (3%)
  between operations  13.5 us (2%)
    all_to_all x1, waiting for transfers between devices, shards(): lax.all_to_all(outgoing, 'sector', split_axis=0, concat_axis=0, tiled=True)  189 us
    psum x1, waiting for transfers between devices, shards(): summed = lax.psum(partial_value, 'term')  90.3 us
    scatter-add x11, other arithmetic, step(): return total.at[rows[:, 2]].add(contract(first, second))  82 us
    gather x11, local copies, waits for them, and re-layouts, step(): first = jnp.take(first_tiles, rows[:, 0], axis=0)  39.8 us
    gather x11, local copies, waits for them, and re-layouts, step(): second = jnp.take(second_tiles, rows[:, 1], axis=0)  38.9 us
    dot_general x8, matrix products, right_product(): jnp.einsum('bvij,bjk->bvik', inter_part, env_part, preferred_element_type...  36.7 us
    all_to_all x1, waiting for transfers between devices, gather_over(): return jnp.concatenate(lax.all_to_all(repeated, name, 0, 0), axis=along)  35.4 us
    transpose x3, local copies, waits for them, and re-layouts, left_product(): jnp.einsum('bij,bvjk->bvik', env_part, wave_part, preferred_element_type=...  16.8 us
  transfers between devices with their start and end apart: 4, of which 3 were waited for; matrix products, arithmetic and copies ran while one was open for 17% of the time, Pallas kernels for 0%

profile of v1, /device:TPU:2, one launch (start us, length us, event | category | flops | bytes accessed | tf_op | source)
XLA Modules:
  0.0 605.8 jit_solution(13523660883666209258)
XLA Ops:
  9.2 10.8 %all-to-all-start.1 = ((bf16[64,1,1,128,128]{4,3,2,1,0:T(8,128)(2,1)}), bf16[64,1,1,128,128]{4,3,2,1,0:T(8,128)(2,1)S(1)}, u32[]{:S(2)}, u32[]{:S(2)}) async-start(bf16[64,1,1,128,128]{4,3,2,1,0:T(8,128)(2,1)} %stack.2), calls=%async_computation.1 | async-start | bytes 4194304 | tf_op jit(solution)/shard_map/all_to_all | solution.py:12
  20.1 6.5 %gather_fusion.4 = bf16[128,2,128,128]{3,2,1,0:T(8,128)(2,1)} fusion(bf16[16,2,128,128]{3,2,1,0:T(8,128)(2,1)S(1)} %copy-done, s32[1024]{0:T(1024)S(1)} %pad_clamp_fusion.4), kind=kCustom, calls=%fused_computation.4 | custom fusion | bytes 16777728 | tf_op jit(solution)/shard_map/jit(_take)/gather | solution.py:45
  26.6 7.5 %select_select_fusion = bf16[128,2,128,128]{3,2,1,0:T(8,128)(2,1)} fusion(bf16[128,2,128,128]{3,2,1,0:T(8,128)(2,1)} %gather_fusion.4, pred[128]{0:T(512)(128)(4,1)S(1)} %get-tuple-element.225, pred[128]{0:T(512)(128)(4,1)S(1)} %get-tuple-element.224), kind=kLoop, calls=%fused_computation.45 | loop fusion | flops 8388608 | bytes 16777472 | tf_op jit(solution)/shard_map/jit(_where)/select_n | solution.py:46
  34.1 35.4 %all-to-all-done.1 = bf16[64,1,1,128,128]{4,3,2,1,0:T(8,128)(2,1)S(1)} async-done(((bf16[64,1,1,128,128]{4,3,2,1,0:T(8,128)(2,1)}), bf16[64,1,1,128,128]{4,3,2,1,0:T(8,128)(2,1)S(1)}, u32[]{:S(2)}, u32[]{:S(2)}) %all-to-all-start.1) | async-done | bytes 2097184 | tf_op jit(solution)/shard_map/all_to_all | solution.py:12
  69.6 7.7 %all-to-all-start = ((bf16[128,2,128,128]{3,2,1,0:T(8,128)(2,1)}), bf16[128,2,128,128]{3,2,1,0:T(8,128)(2,1)}, u32[]{:S(2)}, u32[]{:S(2)}) async-start(bf16[128,2,128,128]{3,2,1,0:T(8,128)(2,1)} %select_select_fusion), calls=%async_computation | async-start | bytes 16777216 | tf_op jit(solution)/shard_map/all_to_all | solution.py:50
  78.1 189.3 %all-to-all-done = bf16[128,2,128,128]{3,2,1,0:T(8,128)(2,1)} async-done(((bf16[128,2,128,128]{3,2,1,0:T(8,128)(2,1)}), bf16[128,2,128,128]{3,2,1,0:T(8,128)(2,1)}, u32[]{:S(2)}, u32[]{:S(2)}) %all-to-all-start) | async-done | bytes 8388640 | tf_op jit(solution)/shard_map/all_to_all | solution.py:50
  269.9 86.2 %while.26 = (s32[]{:T(128)}, f32[32,2,128,128]{3,2,1,0:T(8,128)}, s32[96,3]{0,1:T(4,128)S(1)}, bf16[128,2,128,128]{3,2,1,0:T(8,128)(2,1)}, bf16[64,128,128]{2,1,...) while((s32[]{:T(128)}, f32[32,2,128,128]{3,2,1,0:T(8,128)}, s32[96,3]{0,1:T(4,128)S(1)}, ...), condition=%wide.region_2.4_spmd, body=%wide.region_0.3_spmd.sunk | while | flops 271059520 | bytes 51391044 | solution.py:25
  282.9 5.6 copy.22
  288.6 10.2 %scatter_fusion = f32[32,2,128,128]{3,2,1,0:T(8,128)} fusion(f32[32,2,128,128]{3,2,1,0:T(8,128)} %get-tuple-element.314, s32[32]{0:T(128)S(1)} %get-tuple-element.291, f32[32,2,128,128]{3,2,1,0:T(8,128)} %copy.22), kind=kCustom, calls=%fused_computation.5.clone.1 | custom fusion | flops 1048576 | bytes 12583040 | tf_op jit(solution)/shard_map/while/body/eval_jaxpr/scatter-add | solution.py:23
  311.8 5.6 copy.22
  317.4 10.0 %scatter_fusion = f32[32,2,128,128]{3,2,1,0:T(8,128)} fusion(f32[32,2,128,128]{3,2,1,0:T(8,128)} %get-tuple-element.314, s32[32]{0:T(128)S(1)} %get-tuple-element.291, f32[32,2,128,128]{3,2,1,0:T(8,128)} %copy.22), kind=kCustom, calls=%fused_computation.5.clone.1 | custom fusion | flops 1048576 | bytes 12583040 | tf_op jit(solution)/shard_map/while/body/eval_jaxpr/scatter-add | solution.py:23
  340.5 5.6 copy.22
  346.1 10.0 %scatter_fusion = f32[32,2,128,128]{3,2,1,0:T(8,128)} fusion(f32[32,2,128,128]{3,2,1,0:T(8,128)} %get-tuple-element.314, s32[32]{0:T(128)S(1)} %get-tuple-element.291, f32[32,2,128,128]{3,2,1,0:T(8,128)} %copy.22), kind=kCustom, calls=%fused_computation.5.clone.1 | custom fusion | flops 1048576 | bytes 12583040 | tf_op jit(solution)/shard_map/while/body/eval_jaxpr/scatter-add | solution.py:23
  360.2 145.5 %while.27 = (s32[]{:T(128)}, f32[16,2,128,128]{3,2,1,0:T(8,128)S(1)}, s32[256,3]{0,1:T(4,128)S(1)}, bf16[32,2,128,128]{3,2,1,0:T(8,128)(2,1)}, bf16[64,128,128]{...) while((s32[]{:T(128)}, f32[16,2,128,128]{3,2,1,0:T(8,128)S(1)}, ...), condition=%wide.region_5.7_spmd, body=%wide.region_3.6_spmd.sunk | while | flops 271059520 | bytes 26225168 | solution.py:25
  371.9 6.5 %scatter_fusion.1 = f32[16,2,128,128]{3,2,1,0:T(8,128)S(1)} fusion(f32[16,2,128,128]{3,2,1,0:T(8,128)S(1)} %get-tuple-element.341, s32[32]{0:T(128)S(1)} %get-tuple-element.300, f32[32,2,128,128]{3,2,1,0:T(8,128)} %fusion.34), kind=kCustom, calls=%fused_computation.6.clone.1 | custom fusion | flops 1048576 | bytes 12583040 | tf_op jit(solution)/shard_map/while/body/eval_jaxpr/scatter-add | solution.py:23
  385.5 4.6 fusion.34
  390.1 6.5 %scatter_fusion.1 = f32[16,2,128,128]{3,2,1,0:T(8,128)S(1)} fusion(f32[16,2,128,128]{3,2,1,0:T(8,128)S(1)} %get-tuple-element.341, s32[32]{0:T(128)S(1)} %get-tuple-element.300, f32[32,2,128,128]{3,2,1,0:T(8,128)} %fusion.34), kind=kCustom, calls=%fused_computation.6.clone.1 | custom fusion | flops 1048576 | bytes 12583040 | tf_op jit(solution)/shard_map/while/body/eval_jaxpr/scatter-add | solution.py:23
  408.3 6.5 %scatter_fusion.1 = f32[16,2,128,128]{3,2,1,0:T(8,128)S(1)} fusion(f32[16,2,128,128]{3,2,1,0:T(8,128)S(1)} %get-tuple-element.341, s32[32]{0:T(128)S(1)} %get-tuple-element.300, f32[32,2,128,128]{3,2,1,0:T(8,128)} %fusion.34), kind=kCustom, calls=%fused_computation.6.clone.1 | custom fusion | flops 1048576 | bytes 12583040 | tf_op jit(solution)/shard_map/while/body/eval_jaxpr/scatter-add | solution.py:23
  426.5 6.5 %scatter_fusion.1 = f32[16,2,128,128]{3,2,1,0:T(8,128)S(1)} fusion(f32[16,2,128,128]{3,2,1,0:T(8,128)S(1)} %get-tuple-element.341, s32[32]{0:T(128)S(1)} %get-tuple-element.300, f32[32,2,128,128]{3,2,1,0:T(8,128)} %fusion.34), kind=kCustom, calls=%fused_computation.6.clone.1 | custom fusion | flops 1048576 | bytes 12583040 | tf_op jit(solution)/shard_map/while/body/eval_jaxpr/scatter-add | solution.py:23
  444.7 6.5 %scatter_fusion.1 = f32[16,2,128,128]{3,2,1,0:T(8,128)S(1)} fusion(f32[16,2,128,128]{3,2,1,0:T(8,128)S(1)} %get-tuple-element.341, s32[32]{0:T(128)S(1)} %get-tuple-element.300, f32[32,2,128,128]{3,2,1,0:T(8,128)} %fusion.34), kind=kCustom, calls=%fused_computation.6.clone.1 | custom fusion | flops 1048576 | bytes 12583040 | tf_op jit(solution)/shard_map/while/body/eval_jaxpr/scatter-add | solution.py:23
  462.9 6.5 %scatter_fusion.1 = f32[16,2,128,128]{3,2,1,0:T(8,128)S(1)} fusion(f32[16,2,128,128]{3,2,1,0:T(8,128)S(1)} %get-tuple-element.341, s32[32]{0:T(128)S(1)} %get-tuple-element.300, f32[32,2,128,128]{3,2,1,0:T(8,128)} %fusion.34), kind=kCustom, calls=%fused_computation.6.clone.1 | custom fusion | flops 1048576 | bytes 12583040 | tf_op jit(solution)/shard_map/while/body/eval_jaxpr/scatter-add | solution.py:23
  481.0 6.5 %scatter_fusion.1 = f32[16,2,128,128]{3,2,1,0:T(8,128)S(1)} fusion(f32[16,2,128,128]{3,2,1,0:T(8,128)S(1)} %get-tuple-element.341, s32[32]{0:T(128)S(1)} %get-tuple-element.300, f32[32,2,128,128]{3,2,1,0:T(8,128)} %fusion.34), kind=kCustom, calls=%fused_computation.6.clone.1 | custom fusion | flops 1048576 | bytes 12583040 | tf_op jit(solution)/shard_map/while/body/eval_jaxpr/scatter-add | solution.py:23
  499.2 6.5 %scatter_fusion.1 = f32[16,2,128,128]{3,2,1,0:T(8,128)S(1)} fusion(f32[16,2,128,128]{3,2,1,0:T(8,128)S(1)} %get-tuple-element.341, s32[32]{0:T(128)S(1)} %get-tuple-element.300, f32[32,2,128,128]{3,2,1,0:T(8,128)} %fusion.34), kind=kCustom, calls=%fused_computation.6.clone.1 | custom fusion | flops 1048576 | bytes 12583040 | tf_op jit(solution)/shard_map/while/body/eval_jaxpr/scatter-add | solution.py:23
  507.1 90.3 %all-reduce.2.cloned.1.call-done = f32[16,2,128,128]{3,2,1,0:T(8,128)} async-done(((f32[16,2,128,128]{3,2,1,0:T(8,128)}), f32[16,2,128,128]{3,2,1,0:T(8,128)}) %all-reduce.2.cloned.1.call-update) | async-done | bytes 2097168 | tf_op jit(solution)/shard_map/psum | solution.py:57
  (135 shorter events, 141.0 us)
Async XLA Ops:
  6.5 13.5 %copy-start = (bf16[16,2,128,128]{3,2,1,0:T(8,128)(2,1)S(1)}, bf16[16,2,128,128]{3,2,1,0:T(8,128)(2,1)}, u32[]{:S(2)}) copy-start(bf16[16,2,128,128]{3,2,1,0:T(8,128)(2,1)} %param.12) | copy-start | bytes 3145732
  9.2 10.8 %copy-start.6 = (s32[1,128]{1,0:T(1,128)S(1)}, s32[1,128]{1,0:T(1,128)}, u32[]{:S(2)}) copy-start(s32[1,128]{1,0:T(1,128)} %param.15) | copy-start | bytes 1540
  9.2 60.3 %all-to-all-start.1 = ((bf16[64,1,1,128,128]{4,3,2,1,0:T(8,128)(2,1)}), bf16[64,1,1,128,128]{4,3,2,1,0:T(8,128)(2,1)S(1)}, u32[]{:S(2)}, u32[]{:S(2)}) async-start(bf16[64,1,1,128,128]{4,3,2,1,0:T(8,128)(2,1)} %stack.2), calls=%async_computation.1 | async-start | bytes 4194304 | tf_op jit(solution)/shard_map/all_to_all | solution.py:12
  34.1 44.0 %copy-start.5 = (s32[1,1,96,3]{2,1,3,0:T(1,128)S(1)}, s32[1,1,96,3]{2,1,3,0:T(1,128)}, u32[]{:S(2)}) copy-start(s32[1,1,96,3]{2,1,3,0:T(1,128)} %param.16) | copy-start | bytes 3460
  34.1 44.0 %copy-start.4 = (s32[1,1,256,3]{2,1,3,0:T(1,128)S(1)}, s32[1,1,256,3]{2,1,3,0:T(1,128)}, u32[]{:S(2)}) copy-start(s32[1,1,256,3]{2,1,3,0:T(1,128)} %param.17) | copy-start | bytes 9220
  69.6 197.9 %all-to-all-start = ((bf16[128,2,128,128]{3,2,1,0:T(8,128)(2,1)}), bf16[128,2,128,128]{3,2,1,0:T(8,128)(2,1)}, u32[]{:S(2)}, u32[]{:S(2)}) async-start(bf16[128,2,128,128]{3,2,1,0:T(8,128)(2,1)} %select_select_fusion), calls=%async_computation | async-start | bytes 16777216 | tf_op jit(solution)/shard_map/all_to_all | solution.py:50
  77.3 282.7 %all-gather.2.cloned.1.call-start = ((), (), s32[]{:S(2)}) async-start(), calls=%async_computation.2 | async-start | bytes 2129920 | tf_op jit(solution)/shard_map/all_gather | solution.py:39
  78.0 519.3 %all-reduce.2.cloned.1.call-start = ((), (), s32[]{:S(2)}) async-start(), calls=%async_computation.3 | async-start | bytes 4194304 | tf_op jit(solution)/shard_map/psum | solution.py:57
  269.9 1.3 copy-start.2
  288.6 10.2 %copy-start.3 = (bf16[64,128,128]{2,1,0:T(8,128)(2,1)S(1)}, bf16[64,128,128]{2,1,0:T(8,128)(2,1)}, u32[]{:S(2)}) copy-start(bf16[64,128,128]{2,1,0:T(8,128)(2,1)} %copy-done.2) | copy-start | bytes 6291460 | tf_op jit(solution)/shard_map/while
  298.7 1.3 copy-start.2
  317.4 10.0 %copy-start.3 = (bf16[64,128,128]{2,1,0:T(8,128)(2,1)S(1)}, bf16[64,128,128]{2,1,0:T(8,128)(2,1)}, u32[]{:S(2)}) copy-start(bf16[64,128,128]{2,1,0:T(8,128)(2,1)} %copy-done.2) | copy-start | bytes 6291460 | tf_op jit(solution)/shard_map/while
  327.4 1.3 copy-start.2
  346.1 10.0 %copy-start.3 = (bf16[64,128,128]{2,1,0:T(8,128)(2,1)S(1)}, bf16[64,128,128]{2,1,0:T(8,128)(2,1)}, u32[]{:S(2)}) copy-start(bf16[64,128,128]{2,1,0:T(8,128)(2,1)} %copy-done.2) | copy-start | bytes 6291460 | tf_op jit(solution)/shard_map/while
  505.7 1.3 copy-start.1
Sparse Core Ops, SparseCore 0:
  81.5 99.7 all-gather.1
  507.2 90.0 all-reduce.1
